TPU v7x, 256 devices: a whole 4x4x8 slice. The times are simulated.
256 devices in a mesh: grp: 4 (over x), tp: 32 (over y_lo, z, core), cores: 2 (over y_hi).
Axes of the slice: x: 4, y: 4 (y_hi: 2, y_lo: 2; y = y_hi * 2 + y_lo), z: 8, core: 2. Of those that a mesh axis runs over, the one named last changes fastest.
Arguments:
- tokens: bfloat16 [4096, 8192], P('grp', ('tp', 'cores')), may hold values from -6 to 6
- gate_up_weight: bfloat16 [8192, 2, 16384], P(None, None, ('tp', 'cores')), may hold values from -0.0625 to 0.0625
- down_factor_pool: bfloat16 [64, 8192, 256], P(('tp', 'cores'), 'grp'), may hold values from -0.0625 to 0.0625
- up_factor_pool: bfloat16 [64, 4, 64, 128, 128], P(('tp', 'cores'), 'grp'), may hold values from -0.5 to 0.5
- segment_adapters: int32 [4, 3], replicated, may hold values from 0 to 63
- segment_tile_counts: int32 [4, 3], P('grp'), may hold values from 1 to 4, 8 in all within a row
- adapter_pool_rows: int32 [64], replicated, may hold values from 0 to 63, each once
Outputs:
- hidden: bfloat16 [4096, 16384], P('grp', ('tp', 'cores'))
Inputs may be any that keep to these rules, and one draw needn't show every extreme that they name: `segment_tile_counts`: each row sums to 8. `adapter_pool_rows`: each pool row appears once.
All inputs are finite; a program needn't handle non-finite values.
Results may differ from a plain program's by a relative error of at most 0.0036.
Values may be sent and summed in bfloat16 or wider, within the bound.
No kernel may reach another device: no remote copies, remote signals or barrier semaphores. Data moves between devices by JAX's collectives and lax.ppermute only.
A program may use at most 192 MiB of HBM per device.

v0:
```python
import jax
import jax.numpy as jnp
from jax import lax
from jax.sharding import PartitionSpec as P

TILE = 128
adapter_scale = 0.5


def tile_segments(tile_lengths, tile_count):
    bounds = jnp.cumsum(tile_lengths)
    positions = jnp.arange(tile_count, dtype=jnp.int32)
    return jnp.sum((bounds[None, :] <= positions[:, None]).astype(jnp.int32), axis=1)


def per_device(
    tokens,
    gate_up_weight,
    down_factor_pool,
    up_factor_pool,
    segment_adapters,
    segment_tile_counts,
    adapter_pool_rows,
):
    groups = lax.axis_size("grp")
    device_shares = lax.axis_size(("tp", "cores"))
    group_index = lax.axis_index("grp")
    piece_index = lax.axis_index(("tp", "cores"))
    token_count = tokens.shape[0]
    full_width = tokens.shape[1] * device_shares
    local_hidden_width = gate_up_weight.shape[2]
    twice_rank = down_factor_pool.shape[2]
    rank_size = twice_rank // 2
    share_rows = down_factor_pool.shape[1] // device_shares
    local_count = down_factor_pool.shape[0]
    narrow = local_hidden_width // groups
    local_down_factor = down_factor_pool.reshape(
        local_count, device_shares, share_rows * twice_rank
    )
    local_up_factor = up_factor_pool.reshape(local_count, device_shares, -1)
    a_spread, b_spread = (
        lax.all_to_all(local_down_factor, ("tp", "cores"), split_axis=1, concat_axis=0, tiled=True),
        lax.all_to_all(local_up_factor, ("tp", "cores"), split_axis=1, concat_axis=0, tiled=True),
    )
    a_blocks, b_blocks = (
        lax.all_gather(a_spread, "grp", axis=1, tiled=True),
        lax.all_gather(b_spread, "grp", axis=1, tiled=True),
    )
    own_ids = lax.dynamic_index_in_dim(segment_adapters, group_index, 0, keepdims=False)
    own_slots = jnp.take(adapter_pool_rows, own_ids)
    a_chosen = jnp.take(a_blocks, own_slots, axis=0)
    b_chosen = jnp.take(b_blocks, own_slots, axis=0)
    gathered = lax.all_gather(tokens, ("tp", "cores"), axis=1, tiled=True)
    frozen_output = jnp.dot(
        gathered,
        gate_up_weight.reshape(full_width, 2 * local_hidden_width),
        preferred_element_type=jnp.float32,
    )
    frozen_output = frozen_output.reshape(token_count, 2, local_hidden_width)
    tile_count = token_count // TILE
    tile_seg = tile_segments(segment_tile_counts[0], tile_count)
    a_tiles = jnp.take(a_chosen, tile_seg, axis=0).reshape(
        tile_count, groups * share_rows, twice_rank
    )
    own_features = lax.dynamic_slice_in_dim(
        gathered.reshape(token_count, groups, device_shares, share_rows), piece_index, 1, axis=2
    )
    own_features = own_features.reshape(tile_count, TILE, groups * share_rows)
    partial_shrink = jnp.einsum(
        "tkd,tdr->tkr", own_features, a_tiles, preferred_element_type=jnp.float32
    )
    reduced_input = lax.psum(partial_shrink, ("tp", "cores")).astype(jnp.bfloat16)
    b_tiles = jnp.take(b_chosen, tile_seg, axis=0).reshape(tile_count, groups, rank_size, 2, narrow)
    gate_adapter_delta = jnp.einsum(
        "tkr,tmrw->tkmw",
        reduced_input[:, :, :rank_size],
        b_tiles[:, :, :, 0, :],
        preferred_element_type=jnp.float32,
    )
    up_adapter_delta = jnp.einsum(
        "tkr,tmrw->tkmw",
        reduced_input[:, :, rank_size:],
        b_tiles[:, :, :, 1, :],
        preferred_element_type=jnp.float32,
    )
    gate_combined = frozen_output[:, 0, :] + adapter_scale * gate_adapter_delta.reshape(
        token_count, local_hidden_width
    )
    up_combined = frozen_output[:, 1, :] + adapter_scale * up_adapter_delta.reshape(
        token_count, local_hidden_width
    )
    return (jax.nn.silu(gate_combined) * up_combined).astype(jnp.bfloat16)


def solution(mesh):
    return jax.shard_map(
        per_device,
        mesh=mesh,
        in_specs=(
            P("grp", ("tp", "cores")),
            P(None, None, ("tp", "cores")),
            P(("tp", "cores"), "grp", None),
            P(("tp", "cores"), "grp", None, None, None),
            P(),
            P("grp", None),
            P(),
        ),
        out_specs=P("grp", ("tp", "cores")),
        check_vma=False,
    )
```

profile of v0, /device:TPU:97, one launch (start us, length us, event | category | flops | bytes accessed | tf_op | source)
XLA Modules:
  0.0 831.8 jit_solution(2423148219487207486)
XLA Ops:
  6.5 4.0 reshape.205
  10.5 0.5 broadcast.186
  11.0 7.4 reduce.3
  18.4 0.8 reshape.214
  19.2 39.0 %all_to_all.24 = bf16[64,2,4096]{2,1,0:T(2,128)(2,1)S(1)} all-to-all(bf16[64,2,4096]{2,1,0:T(2,128)(2,1)S(1)} %reshape.214), channel_id=1, replica_groups=mesh['grp'=4,'tp'=32,'cores'=2] {'tp','cores'}, dimensions={0} | all-to-all | bytes 2097152 | tf_op jit(solution)/shard_map/all_to_all | solution.py:42
  58.3 3.5 reshape.215
  61.8 10.1 %reshape.206 = bf16[1,64,16384]{2,0,1:T(2,128)(2,1)} reshape(bf16[1,1,64,128,128]{4,3,2,1,0:T(8,128)(2,1)} %param.10) | data formatting | bytes 4194304 | tf_op jit(solution)/shard_map/reshape | solution.py:40
  71.9 13.7 %reduce.2 = bf16[64,16384]{1,0:T(8,128)(2,1)S(1)} reduce(bf16[64,1,16384]{2,1,0:T(2,128)(2,1)} %bitcast.76, bf16[]{:T(256)} %broadcast.186), dimensions={1}, to_apply=%bitcast.67.reduce_sub_computation | reduce | bytes 4194306
  85.6 2.8 reshape.212
  88.4 57.5 %all_to_all.25 = bf16[64,2,8192]{2,1,0:T(2,128)(2,1)S(1)} all-to-all(bf16[64,2,8192]{2,1,0:T(2,128)(2,1)} %reshape.212), channel_id=1, replica_groups=mesh['grp'=4,'tp'=32,'cores'=2] {'tp','cores'}, dimensions={0} | all-to-all | bytes 4194304 | tf_op jit(solution)/shard_map/all_to_all | solution.py:43
  145.8 6.7 reshape.213
  152.6 0.7 all-gather.6.cloned.1.call-update
  153.3 0.2 reduce-window.8
  153.5 8.0 copy.65
  161.5 12.2 %copy.48 = bf16[512,8192]{1,0:T(8,128)(2,1)} copy(bf16[512,8192]{0,1:T(8,128)(2,1)} %bitcast.74) | data formatting | bytes 16777216 | tf_op jit(solution)/shard_map/dot_general | solution.py:54
  173.8 0.6 gather_fusion
  174.4 0.1 convert_reduce_fusion
  174.6 27.3 %reduce = bf16[64,32768]{1,0:T(8,128)(2,1)} reduce(bf16[1,64,32768]{2,0,1:T(2,128)(2,1)} %all-gather.8.cloned.1.call-done, bf16[]{:T(256)} %constant.100), dimensions={0}, to_apply=%all-gather.reduce_sub_computation | reduce | bytes 8388610 | tf_op jit(solution)/shard_map/all_gather | solution.py:46
  201.9 7.9 reshape.198
  209.8 3.0 gather_fusion.1
  212.8 0.2 broadcast_select_fusion.2
  213.0 1.0 gather_fusion.2
  214.0 1.2 gather.30
  215.1 91.7 %all-gather.10.cloned.1.call-done = bf16[1,64,65536]{2,0,1:T(2,128)(2,1)} async-done(((bf16[1,64,16384]{2,0,1:T(2,128)(2,1)}), bf16[1,64,65536]{2,0,1:T(2,128)(2,1)}) %all-gather.10.cloned.1.call-update) | async-done | bytes 8388624 | tf_op jit(solution)/shard_map/all_gather | solution.py:47
  306.9 52.7 %reduce.1 = bf16[64,65536]{1,0:T(8,128)(2,1)} reduce(bf16[1,64,65536]{2,0,1:T(2,128)(2,1)} %all-gather.10.cloned.1.call-done, bf16[]{:T(256)} %constant.100), dimensions={0}, to_apply=%all-gather.1.reduce_sub_computation | reduce | bytes 16777218 | tf_op jit(solution)/shard_map/all_gather | solution.py:47
  359.5 11.7 %reshape.199 = bf16[64,4,16384]{2,1,0:T(4,128)(2,1)} reshape(bf16[64,65536]{1,0:T(8,128)(2,1)} %reduce.1) | data formatting | bytes 16777216 | tf_op jit(solution)/shard_map/all_gather | solution.py:47
  371.2 4.4 gather_fusion.3
  375.6 0.2 broadcast_select_fusion.1
  375.9 1.4 gather_fusion.4
  377.3 1.7 reshape.207
  379.0 1.5 copy.54
  380.5 0.2 broadcast_select_fusion
  380.7 0.9 fusion.19
  381.6 129.9 %all-gather.6.cloned.1.call-done = bf16[1024,8192]{1,0:T(8,128)(2,1)} async-done(((bf16[1024,128]{1,0:T(8,128)(2,1)}), bf16[1024,8192]{1,0:T(8,128)(2,1)}) %all-gather.6.cloned.1.call-update) | async-done | bytes 16777232 | tf_op jit(solution)/shard_map/all_gather | solution.py:53
  511.4 22.4 %copy.49 = bf16[1024,8192]{0,1:T(8,128)(2,1)} copy(bf16[1024,8192]{1,0:T(8,128)(2,1)} %all-gather.6.cloned.1.call-done) | data formatting | bytes 33554432 | tf_op jit(solution)/shard_map/all_gather | solution.py:53
  533.9 1.0 constant_dynamic-slice_fusion.1
  534.9 0.4 fusion.6
  535.3 266.7 %all-reduce.1 = bf16[8,128,256]{2,1,0:T(8,128)(2,1)S(1)} all-reduce(f32[8,128,256]{2,1,0:T(8,128)S(1)} %fusion.6), channel_id=1, replica_groups=mesh['grp'=4,'tp'=32,'cores'=2] {'tp','cores'}, use_global_device_ids=true, to_apply=%region_2.3 | all-reduce | flops 262144 | bytes 1572864 | tf_op jit(solution)/shard_map/psum | solution.py:72
  802.0 0.3 fusion.9
  802.3 0.5 copy-done.3
  802.9 0.9 copy.62
  803.8 2.2 reshape.209
  806.0 1.4 fusion.11
  807.4 0.1 broadcast_multiply_fusion.1
  807.5 0.9 copy.61
  808.4 1.2 reshape.208
  809.6 14.5 %fusion = f32[1024,2,256]{2,0,1:T(8,128)S(1)} fusion(bf16[2,256,8192]{2,1,0:T(8,128)(2,1)} %bitcast.79, bf16[1024,8192]{1,0:T(8,128)(2,1)} %all-gather.6.cloned.1.call-done), kind=kOutput, calls=%fused_computation.5 | convolution fusion | flops 8589934592 | bytes 27262976 | tf_op jit(solution)/shard_map/dot_general | solution.py:54
  824.1 1.1 fusion.4
  (29 shorter events, 0.4 us)
Async XLA Ops:
  6.5 167.2 %copy-start = (s32[64]{0:T(128)S(1)}, s32[64]{0:T(128)}, u32[]{:S(2)}) copy-start(s32[64]{0:T(128)} %param.13) | copy-start | bytes 772
  6.5 168.1 %all-gather.8.cloned.1.call-start = ((), (), s32[]{:S(2)}) async-start(), calls=%async_computation.3 | async-start | bytes 10485760 | tf_op jit(solution)/shard_map/all_gather | solution.py:46
  61.8 245.1 %all-gather.10.cloned.1.call-start = ((), (), s32[]{:S(2)}) async-start(), calls=%async_computation.4 | async-start | bytes 20971520 | tf_op jit(solution)/shard_map/all_gather | solution.py:47
  88.4 65.0 %copy-start.6 = (s32[1,3]{1,0:T(1,128)S(1)}, s32[1,3]{1,0:T(1,128)}, u32[]{:S(2)}) copy-start(s32[1,3]{1,0:T(1,128)} %param.12) | copy-start | bytes 40
  152.6 358.9 %all-gather.6.cloned.1.call-start = ((), (), s32[]{:S(2)}) async-start(), calls=%async_computation.2 | async-start | bytes 17039360 | tf_op jit(solution)/shard_map/all_gather | solution.py:53
  161.5 12.2 %copy-start.5 = (s32[4,3]{1,0:T(4,128)S(1)}, s32[4,3]{1,0:T(4,128)}, u32[]{:S(2)}) copy-start(s32[4,3]{1,0:T(4,128)} %param.11) | copy-start | bytes 148
  381.6 153.3 %copy-start.4 = (bf16[8,128,256]{2,1,0:T(8,128)(2,1)S(1)}, bf16[8,128,256]{2,1,0:T(8,128)(2,1)}, u32[]{:S(2)}) copy-start(bf16[8,128,256]{2,1,0:T(8,128)(2,1)} %gather.30) | copy-start | bytes 1572868
  802.0 0.8 copy-start.3
  809.6 14.6 %copy-start.2 = (f32[1024,256]{1,0:T(8,128)S(1)}, f32[1024,256]{1,0:T(8,128)}, u32[]{:S(2)}) copy-start(f32[1024,256]{1,0:T(8,128)} %reshape.209) | copy-start | bytes 3145732
  809.6 15.7 %copy-start.1 = (s32[64]{0:T(128)S(1)}, s32[64]{0:T(128)}, u32[]{:S(2)}) copy-start(s32[64]{0:T(128)} %param.13) | copy-start | bytes 772
Sparse Core Ops, SparseCore 0:
  61.9 83.1 all-gather.7
  152.7 154.1 all-gather.9
  308.6 202.7 all-gather.5
where the time goes:
time: 834 us; the launch traced here: 832 us
  blocking collectives  363 us (44%)
  waiting for transfers between devices  222 us (27%)
  local copies, waits for them, and re-layouts  113 us (14%)
  other arithmetic  103 us (12%)
  matrix products  16.6 us (2%)
  between operations  13.4 us (2%)
    psum x1, blocking collectives, per_device(): lax.psum(partial_shrink, ('tp', 'cores')).astype(jnp.bfloat16)  267 us
    all_gather x1, waiting for transfers between devices, per_device(): gathered = lax.all_gather(tokens, ('tp', 'cores'), axis=1, tiled=True)  130 us
    all_gather x1, waiting for transfers between devices, per_device(): lax.all_gather(b_spread, 'grp', axis=1, tiled=True)  91.7 us
    all_to_all x1, blocking collectives, per_device(): lax.all_to_all(local_up_factor, ('tp', 'cores'), split_axis=1, concat_axi...  57.5 us
    all_gather x1, other arithmetic, per_device(): lax.all_gather(b_spread, 'grp', axis=1, tiled=True)  52.7 us
    all_to_all x1, blocking collectives, per_device(): lax.all_to_all(local_down_factor, ('tp', 'cores'), split_axis=1, concat_a...  39 us
    all_gather x1, other arithmetic, per_device(): lax.all_gather(a_spread, 'grp', axis=1, tiled=True)  27.3 us
    unnamed x21, local copies, waits for them, and re-layouts  22.9 us
  transfers between devices with their start and end apart: 3, of which 2 were waited for; matrix products, arithmetic and copies ran while one was open for 20% of the time, Pallas kernels for 0%

commit v1 on v0

--- a/solution.py
+++ b/solution.py
@@ -69,7 +69,7 @@
     partial_shrink = jnp.einsum(
         "tkd,tdr->tkr", own_features, a_tiles, preferred_element_type=jnp.float32
     )
-    reduced_input = lax.psum(partial_shrink, ("tp", "cores")).astype(jnp.bfloat16)
+    reduced_input = lax.psum(lax.psum(partial_shrink, "cores"), "tp").astype(jnp.bfloat16)
     b_tiles = jnp.take(b_chosen, tile_seg, axis=0).reshape(tile_count, groups, rank_size, 2, narrow)
     gate_adapter_delta = jnp.einsum(
         "tkr,tmrw->tkmw",

time: 834 us -> 727 us (0.87)
  the two profiles are of different devices: /device:TPU:97 before, /device:TPU:2 now
where the time goes in v1:
time: 727 us; the launch traced here: 725 us
  waiting for transfers between devices  261 us (36%)
  blocking collectives  214 us (29%)
  local copies, waits for them, and re-layouts  112 us (15%)
  other arithmetic  105 us (14%)
  matrix products  18.9 us (3%)
  between operations  13.4 us (2%)
    all_gather x1, waiting for transfers between devices, per_device(): gathered = lax.all_gather(tokens, ('tp', 'cores'), axis=1, tiled=True)  129 us
    psum x1, blocking collectives, per_device(): lax.psum(lax.psum(partial_shrink, 'cores'), 'tp').astype(jnp.bfloat16)  118 us
    all_gather x1, waiting for transfers between devices, per_device(): lax.all_gather(b_spread, 'grp', axis=1, tiled=True)  94 us
    all_to_all x1, blocking collectives, per_device(): lax.all_to_all(local_up_factor, ('tp', 'cores'), split_axis=1, concat_axi...  56 us
    all_gather x1, other arithmetic, per_device(): lax.all_gather(b_spread, 'grp', axis=1, tiled=True)  52.7 us
    all_to_all x1, blocking collectives, per_device(): lax.all_to_all(local_down_factor, ('tp', 'cores'), split_axis=1, concat_a...  39.8 us
    psum x1, waiting for transfers between devices, per_device(): lax.psum(partial_shrink, 'cores')  37.3 us
    all_gather x1, other arithmetic, per_device(): lax.all_gather(a_spread, 'grp', axis=1, tiled=True)  27.4 us
  transfers between devices with their start and end apart: 4, of which 3 were waited for; matrix products, arithmetic and copies ran while one was open for 26% of the time, Pallas kernels for 0%

profile of v1, /device:TPU:2, one launch (start us, length us, event | category | flops | bytes accessed | tf_op | source)
XLA Modules:
  0.0 724.6 jit_solution(8085243916009657662)
XLA Ops:
  6.5 4.0 reshape.205
  10.5 0.5 broadcast.186
  11.0 7.4 %reduce.3 = bf16[64,8192]{1,0:T(8,128)(2,1)S(1)} reduce(bf16[64,1,8192]{2,1,0:T(2,128)(2,1)S(1)} %bitcast.81, bf16[]{:T(256)} %broadcast.186), dimensions={1}, to_apply=%bitcast.69.reduce_sub_computation | reduce | bytes 2097154
  18.4 0.8 reshape.214
  19.2 39.8 %all_to_all.24 = bf16[64,2,4096]{2,1,0:T(2,128)(2,1)S(1)} all-to-all(bf16[64,2,4096]{2,1,0:T(2,128)(2,1)S(1)} %reshape.214), channel_id=1, replica_groups=mesh['grp'=4,'tp'=32,'cores'=2] {'tp','cores'}, dimensions={0} | all-to-all | bytes 2097152 | tf_op jit(solution)/shard_map/all_to_all | solution.py:42
  59.0 3.5 reshape.215
  62.5 10.1 %reshape.206 = bf16[1,64,16384]{2,0,1:T(2,128)(2,1)} reshape(bf16[1,1,64,128,128]{4,3,2,1,0:T(8,128)(2,1)} %param.10) | data formatting | bytes 4194304 | tf_op jit(solution)/shard_map/reshape | solution.py:40
  72.6 13.7 %reduce.2 = bf16[64,16384]{1,0:T(8,128)(2,1)S(1)} reduce(bf16[64,1,16384]{2,1,0:T(2,128)(2,1)} %bitcast.76, bf16[]{:T(256)} %broadcast.186), dimensions={1}, to_apply=%bitcast.67.reduce_sub_computation | reduce | bytes 4194306
  86.3 2.8 reshape.212
  89.1 56.0 %all_to_all.25 = bf16[64,2,8192]{2,1,0:T(2,128)(2,1)S(1)} all-to-all(bf16[64,2,8192]{2,1,0:T(2,128)(2,1)} %reshape.212), channel_id=1, replica_groups=mesh['grp'=4,'tp'=32,'cores'=2] {'tp','cores'}, dimensions={0} | all-to-all | bytes 4194304 | tf_op jit(solution)/shard_map/all_to_all | solution.py:43
  145.1 6.7 reshape.213
  151.9 0.7 all-gather.6.cloned.1.call-update
  152.6 0.2 reduce-window.8
  152.8 8.0 %copy.65 = bf16[1024,8,2,256]{3,1,2,0:T(8,128)(2,1)} copy(bf16[1024,8,2,256]{3,2,1,0:T(2,128)(2,1)} %bitcast.78) | data formatting | bytes 16777216
  160.8 11.7 %copy.48 = bf16[512,8192]{1,0:T(8,128)(2,1)} copy(bf16[512,8192]{0,1:T(8,128)(2,1)} %bitcast.74) | data formatting | bytes 16777216 | tf_op jit(solution)/shard_map/dot_general | solution.py:54
  172.6 0.6 gather_fusion
  173.2 0.1 convert_reduce_fusion
  173.4 27.4 %reduce = bf16[64,32768]{1,0:T(8,128)(2,1)} reduce(bf16[1,64,32768]{2,0,1:T(2,128)(2,1)} %all-gather.8.cloned.1.call-done, bf16[]{:T(256)} %constant.100), dimensions={0}, to_apply=%all-gather.reduce_sub_computation | reduce | bytes 8388610 | tf_op jit(solution)/shard_map/all_gather | solution.py:46
  200.8 7.9 %reshape.198 = bf16[64,4,8192]{2,1,0:T(4,128)(2,1)} reshape(bf16[64,32768]{1,0:T(8,128)(2,1)} %reduce) | data formatting | bytes 8388608 | tf_op jit(solution)/shard_map/all_gather | solution.py:46
  208.6 3.0 gather_fusion.1
  211.6 0.2 broadcast_select_fusion.2
  211.8 1.0 gather_fusion.2
  212.8 1.2 gather.30
  213.9 94.0 %all-gather.10.cloned.1.call-done = bf16[1,64,65536]{2,0,1:T(2,128)(2,1)} async-done(((bf16[1,64,16384]{2,0,1:T(2,128)(2,1)}), bf16[1,64,65536]{2,0,1:T(2,128)(2,1)}) %all-gather.10.cloned.1.call-update) | async-done | bytes 8388624 | tf_op jit(solution)/shard_map/all_gather | solution.py:47
  308.0 52.7 %reduce.1 = bf16[64,65536]{1,0:T(8,128)(2,1)} reduce(bf16[1,64,65536]{2,0,1:T(2,128)(2,1)} %all-gather.10.cloned.1.call-done, bf16[]{:T(256)} %constant.100), dimensions={0}, to_apply=%all-gather.1.reduce_sub_computation | reduce | bytes 16777218 | tf_op jit(solution)/shard_map/all_gather | solution.py:47
  360.6 11.7 %reshape.199 = bf16[64,4,16384]{2,1,0:T(4,128)(2,1)} reshape(bf16[64,65536]{1,0:T(8,128)(2,1)} %reduce.1) | data formatting | bytes 16777216 | tf_op jit(solution)/shard_map/all_gather | solution.py:47
  372.3 4.4 gather_fusion.3
  376.7 0.2 broadcast_select_fusion.1
  377.0 1.4 gather_fusion.4
  378.4 1.7 reshape.207
  380.1 1.5 copy.54
  381.6 0.2 broadcast_select_fusion
  381.7 0.9 fusion.19
  382.6 128.9 %all-gather.6.cloned.1.call-done = bf16[1024,8192]{1,0:T(8,128)(2,1)} async-done(((bf16[1024,128]{1,0:T(8,128)(2,1)}), bf16[1024,8192]{1,0:T(8,128)(2,1)}) %all-gather.6.cloned.1.call-update) | async-done | bytes 16777232 | tf_op jit(solution)/shard_map/all_gather | solution.py:53
  511.5 22.4 %copy.49 = bf16[1024,8192]{0,1:T(8,128)(2,1)} copy(bf16[1024,8192]{1,0:T(8,128)(2,1)} %all-gather.6.cloned.1.call-done) | data formatting | bytes 33554432 | tf_op jit(solution)/shard_map/all_gather | solution.py:53
  533.9 1.0 constant_dynamic-slice_fusion.1
  535.0 1.3 fusion.6
  536.3 15.8 %fusion = f32[1024,2,256]{2,0,1:T(8,128)} fusion(bf16[2,256,8192]{2,1,0:T(8,128)(2,1)} %bitcast.79, bf16[1024,8192]{1,0:T(8,128)(2,1)} %all-gather.6.cloned.1.call-done), kind=kOutput, calls=%fused_computation.5 | convolution fusion | flops 8589934592 | bytes 27262976 | tf_op jit(solution)/shard_map/dot_general | solution.py:54
  552.2 37.3 %all-reduce.3.cloned.1.call-done = f32[8,128,256]{2,1,0:T(8,128)} async-done(((f32[8,128,256]{2,1,0:T(8,128)}), f32[8,128,256]{2,1,0:T(8,128)}) %all-reduce.3.cloned.1.call-update) | async-done | bytes 1048592 | tf_op jit(solution)/shard_map/psum | solution.py:72
  589.5 118.0 %all-reduce.4 = bf16[8,128,256]{2,1,0:T(8,128)(2,1)S(1)} all-reduce(f32[8,128,256]{2,1,0:T(8,128)} %all-reduce.3.cloned.1.call-done), channel_id=1, replica_groups=mesh['grp'=4,'tp'=32,'cores'=2] {'tp'}, use_global_device_ids=true, to_apply=%region_3.4 | all-reduce | flops 262144 | bytes 1572864 | tf_op jit(solution)/shard_map/psum | solution.py:72
  707.5 0.3 fusion.9
  707.8 0.5 copy-done.2
  708.4 0.9 copy.62
  709.3 2.2 reshape.209
  711.5 1.4 fusion.11
  713.0 0.9 copy.61
  713.9 1.2 reshape.208
  715.0 3.1 fusion.4
  (30 shorter events, 0.5 us)
Async XLA Ops:
  6.5 166.0 %copy-start = (s32[64]{0:T(128)S(1)}, s32[64]{0:T(128)}, u32[]{:S(2)}) copy-start(s32[64]{0:T(128)} %param.13) | copy-start | bytes 772
  6.5 166.8 %all-gather.8.cloned.1.call-start = ((), (), s32[]{:S(2)}) async-start(), calls=%async_computation.4 | async-start | bytes 10485760 | tf_op jit(solution)/shard_map/all_gather | solution.py:46
  62.5 245.5 %all-gather.10.cloned.1.call-start = ((), (), s32[]{:S(2)}) async-start(), calls=%async_computation.5 | async-start | bytes 20971520 | tf_op jit(solution)/shard_map/all_gather | solution.py:47
  89.1 63.5 %copy-start.5 = (s32[1,3]{1,0:T(1,128)S(1)}, s32[1,3]{1,0:T(1,128)}, u32[]{:S(2)}) copy-start(s32[1,3]{1,0:T(1,128)} %param.12) | copy-start | bytes 40
  151.8 359.7 %all-gather.6.cloned.1.call-start = ((), (), s32[]{:S(2)}) async-start(), calls=%async_computation.2 | async-start | bytes 17039360 | tf_op jit(solution)/shard_map/all_gather | solution.py:53
  152.6 436.9 %all-reduce.3.cloned.1.call-start = ((), (), s32[]{:S(2)}) async-start(), calls=%async_computation.3 | async-start | bytes 2097152 | tf_op jit(solution)/shard_map/psum | solution.py:72
  160.8 11.7 %copy-start.4 = (s32[4,3]{1,0:T(4,128)S(1)}, s32[4,3]{1,0:T(4,128)}, u32[]{:S(2)}) copy-start(s32[4,3]{1,0:T(4,128)} %param.11) | copy-start | bytes 148
  382.6 152.3 %copy-start.3 = (bf16[8,128,256]{2,1,0:T(8,128)(2,1)S(1)}, bf16[8,128,256]{2,1,0:T(8,128)(2,1)}, u32[]{:S(2)}) copy-start(bf16[8,128,256]{2,1,0:T(8,128)(2,1)} %gather.30) | copy-start | bytes 1572868
  707.5 0.8 copy-start.2
  708.4 9.7 %copy-start.1 = (s32[64]{0:T(128)S(1)}, s32[64]{0:T(128)}, u32[]{:S(2)}) copy-start(s32[64]{0:T(128)} %param.13) | copy-start | bytes 772
Sparse Core Ops, SparseCore 0:
  62.6 83.5 all-gather.7
  151.9 155.9 all-gather.9
  309.7 201.7 all-gather.5
  536.5 52.9 all-reduce.2
